TPU v7x, 32 devices: a whole 2x2x4 slice. The times are simulated.
32 devices in a mesh: parts: 2 (over y), seq: 4 (over z), head: 2 (over x), fsdp: 2 (over core).
Axes of the slice: x: 2, y: 2, z: 4, core: 2. Of those that a mesh axis runs over, the one named last changes fastest.
Arguments:
- frames: bfloat16 [2048, 1024], P(('parts', 'seq', 'head', 'fsdp')), parts along dimension 0, may hold values from -24 to 24
- length: int32 [2], P('parts'), parts along dimension 0, may hold values from 512 to 1024
- ln1_gain: float32 [1024], replicated, may hold values from 0.1 to 1.9
- w_query: bfloat16 [1024, 1024], P('seq', ('head', 'fsdp')), may hold values from -0.2 to 0.2
- w_key: bfloat16 [1024, 1024], P('seq', ('head', 'fsdp')), may hold values from -3 to 3
- w_value: bfloat16 [1024, 1024], P('seq', ('head', 'fsdp')), may hold values from -0.375 to 0.375
- w_out: bfloat16 [1024, 1024], P(('head', 'fsdp'), 'seq'), may hold values from -0.1875 to 0.1875
- ln2_gain: float32 [1024], replicated, may hold values from 0.1 to 1.9
- pw1_value: bfloat16 [1024, 1024], P('seq', ('head', 'fsdp')), may hold values from -0.1875 to 0.1875
- pw1_gate: bfloat16 [1024, 1024], P('seq', ('head', 'fsdp')), may hold values from -0.375 to 0.375
- depth_kernel: float32 [9, 1024], P(None, ('head', 'fsdp')), may hold values from -2 to 2
- bn_scale: float32 [1024], P(('head', 'fsdp')), may hold values from 0.1 to 1.9
- bn_shift: float32 [1024], P(('head', 'fsdp')), may hold values from -3 to 3
- pw2: bfloat16 [1024, 1024], P(('head', 'fsdp'), 'seq'), may hold values from -0.1875 to 0.1875
Outputs:
- encoded: bfloat16 [2048, 1024], P(('parts', 'seq', 'head', 'fsdp')), parts along dimension 0
There are 2 independent parts, one for each index of `parts`. A program takes and returns all parts, laid end to end along the dimension named above; an argument that names none is the same for every part. Nothing has to cross between parts.
All inputs are finite; a program needn't handle non-finite values.
Results may differ from a plain program's by a relative error of at most 0.012.
The roundings to bfloat16 on the way count: a program that leaves them out, or rounds other values in their place, can miss the bound.
Values may be sent and summed in bfloat16 or wider, within the bound.
No kernel may reach another device: no remote copies, remote signals or barrier semaphores. Data moves between devices by JAX's collectives and lax.ppermute only.
A program may use at most 64 MiB of HBM per device.

v0:
```python
import math
import jax
import jax.numpy as jnp
from jax import lax
from jax.sharding import PartitionSpec as P

KERNEL = 9
HD = 128


def with_halo(block, sides, width):
    for axis, dim in sides:
        count = lax.axis_size(axis)
        forward = [(i, i + 1) for i in range(count - 1)]
        backward = [(target, source) for source, target in forward]
        low = lax.ppermute(
            lax.slice_in_dim(block, block.shape[dim] - width, None, axis=dim), axis, forward
        )
        high = lax.ppermute(lax.slice_in_dim(block, 0, width, axis=dim), axis, backward)
        block = jnp.concatenate([low, block, high], axis=dim)
    return block


def layer_norm(values_in, gain_vec):
    center = jnp.mean(values_in, axis=-1, keepdims=True)
    shifted = values_in - center
    spread = jnp.mean(shifted * shifted, axis=-1, keepdims=True)
    return shifted * lax.rsqrt(spread + 1e-05) * gain_vec


def shards(
    frames,
    length,
    ln1_gain,
    w_query,
    w_key,
    w_value,
    w_out,
    ln2_gain,
    pw1_value,
    pw1_gate,
    depth_kernel,
    bn_scale,
    bn_shift,
    pw2,
):
    group_size = lax.axis_size(("head", "fsdp"))
    my_rows = frames.shape[0]
    block_rows = my_rows * group_size
    head_cols = w_query.shape[1]
    heads_here = head_cols // HD
    seq_start = lax.axis_index("seq") * block_rows
    valid_len = length[0]
    score_scale = 1.0 / math.sqrt(HD)
    full_query, full_key, full_value, value_cols, gate_cols = (
        lax.all_gather(w_query, "seq", axis=0, tiled=True),
        lax.all_gather(w_key, "seq", axis=0, tiled=True),
        lax.all_gather(w_value, "seq", axis=0, tiled=True),
        lax.all_gather(pw1_value, "seq", axis=0, tiled=True),
        lax.all_gather(pw1_gate, "seq", axis=0, tiled=True),
    )
    out_rows, down_rows = (
        lax.all_gather(w_out, "seq", axis=1, tiled=True),
        lax.all_gather(pw2, "seq", axis=1, tiled=True),
    )
    projector = jnp.concatenate((full_query, full_key, full_value), axis=1)
    source = frames.astype(jnp.float32)
    normed = layer_norm(source, ln1_gain).astype(jnp.bfloat16)
    projected = jnp.dot(
        lax.all_gather(normed, ("head", "fsdp"), axis=0, tiled=True),
        projector,
        preferred_element_type=jnp.float32,
    ).astype(jnp.bfloat16)
    queries = projected[:, :head_cols].reshape(block_rows, heads_here, HD)
    keys_here = projected[:, head_cols : 2 * head_cols]
    values_here = projected[:, 2 * head_cols :]
    initial = (
        jnp.full((heads_here, block_rows), -1e30, jnp.float32),
        jnp.zeros((heads_here, block_rows), jnp.float32),
        jnp.zeros((heads_here, block_rows, HD), jnp.float32),
    )
    key_piece = lax.all_gather(keys_here, "seq", axis=0, tiled=True)
    value_piece = lax.all_gather(values_here, "seq", axis=0, tiled=True)
    row_count = key_piece.shape[0]
    block_size = math.gcd(row_count, 512)
    block_count = row_count // block_size
    key_blocks = key_piece.reshape(block_count, block_size, heads_here, HD)
    value_blocks = value_piece.reshape(block_count, block_size, heads_here, HD)
    places = jnp.arange(row_count, dtype=jnp.int32).reshape(block_count, block_size)

    def advance(inner_state, block_item):
        key_block, value_block, place = block_item
        peak_score, weight_sum, weighted = inner_state
        scores = (
            jnp.einsum("qhd,khd->hqk", queries, key_block, preferred_element_type=jnp.float32)
            * score_scale
        )
        scores = jnp.where((place < valid_len)[None, None, :], scores, -jnp.inf)
        new_peak = jnp.maximum(peak_score, jnp.max(scores, axis=2))
        factor = jnp.exp(peak_score - new_peak)
        weights = jnp.exp(scores - new_peak[:, :, None])
        weight_sum = weight_sum * factor + jnp.sum(weights, axis=2)
        weighted = weighted * factor[:, :, None] + jnp.einsum(
            "hqk,khd->hqd",
            weights.astype(jnp.bfloat16),
            value_block,
            preferred_element_type=jnp.float32,
        )
        return ((new_peak, weight_sum, weighted), None)

    result, unused = lax.scan(advance, initial, (key_blocks, value_blocks, places))
    peak_score, weight_sum, weighted = result
    context = (
        (weighted / weight_sum[:, :, None])
        .astype(jnp.bfloat16)
        .transpose(1, 0, 2)
        .reshape(block_rows, head_cols)
    )
    attended = lax.psum_scatter(
        jnp.dot(context, out_rows, preferred_element_type=jnp.float32).astype(jnp.bfloat16),
        ("head", "fsdp"),
        scatter_dimension=0,
        tiled=True,
    ).astype(jnp.float32)
    middle = source + attended
    normed_two = layer_norm(middle, ln2_gain).astype(jnp.bfloat16)
    piece = lax.all_gather(normed_two, ("head", "fsdp"), axis=0, tiled=True)
    value_part = jnp.dot(piece, value_cols, preferred_element_type=jnp.float32)
    gate_part = jnp.dot(piece, gate_cols, preferred_element_type=jnp.float32)
    places = seq_start + jnp.arange(piece.shape[0], dtype=jnp.int32)
    gated_rows = jnp.where(
        (places < valid_len)[:, None], value_part * jax.nn.sigmoid(gate_part), 0.0
    ).astype(jnp.bfloat16)
    rim_width = (KERNEL - 1) // 2
    padded = with_halo(gated_rows, (("seq", 0),), rim_width).astype(jnp.float32)
    depth_sum = depth_kernel[0] * padded[0:block_rows]
    for offset in range(1, KERNEL):
        depth_sum = depth_sum + depth_kernel[offset] * padded[offset : offset + block_rows]
    shifted = depth_sum * bn_scale + bn_shift
    active = (shifted * jax.nn.sigmoid(shifted)).astype(jnp.bfloat16)
    conv_part = lax.psum_scatter(
        jnp.dot(active, down_rows, preferred_element_type=jnp.float32).astype(jnp.bfloat16),
        ("head", "fsdp"),
        scatter_dimension=0,
        tiled=True,
    ).astype(jnp.float32)
    return (middle + conv_part).astype(jnp.bfloat16)


def solution(mesh):
    in_specs = (
        P(("parts", "seq", "head", "fsdp"), None),
        P("parts"),
        P(),
        P("seq", ("head", "fsdp")),
        P("seq", ("head", "fsdp")),
        P("seq", ("head", "fsdp")),
        P(("head", "fsdp"), "seq"),
        P(),
        P("seq", ("head", "fsdp")),
        P("seq", ("head", "fsdp")),
        P(None, ("head", "fsdp")),
        P(("head", "fsdp")),
        P(("head", "fsdp")),
        P(("head", "fsdp"), "seq"),
    )
    out_specs = P(("parts", "seq", "head", "fsdp"), None)
    return jax.shard_map(shards, mesh=mesh, in_specs=in_specs, out_specs=out_specs, check_vma=False)
```

profile of v0, /device:TPU:0, one launch (start us, length us, event | category | flops | bytes accessed | tf_op | source)
XLA Modules:
  0.0 217.0 jit_solution(8973462292048037482)
XLA Ops:
  6.6 1.1 convert_reduce_fusion
  7.7 1.1 fusion.24
  8.8 1.0 fusion.26
  9.8 8.8 %all_gather.33 = bf16[256,1024]{1,0:T(8,128)(2,1)S(1)} all-gather(bf16[64,1024]{1,0:T(8,128)(2,1)S(1)} %fusion.26), channel_id=1, replica_groups=mesh['parts'=2,'seq'=4,'head'=2,'fsdp'=2] {'head','fsdp'}, dimensions={0}, use_global_device_ids=true | all-gather | bytes 655360 | tf_op jit(solution)/shard_map/all_gather | solution.py:70
  18.6 16.3 %all_gather.34 = bf16[1024,256]{1,0:T(8,128)(2,1)S(1)} all-gather(bf16[256,256]{1,0:T(8,128)(2,1)S(1)} %copy-done.2), channel_id=1, replica_groups=mesh['parts'=2,'seq'=4,'head'=2,'fsdp'=2] {'seq'}, dimensions={0}, use_global_device_ids=true | all-gather | bytes 655360 | tf_op jit(solution)/shard_map/all_gather | solution.py:56
  34.9 15.9 %all_gather.35 = bf16[1024,256]{1,0:T(8,128)(2,1)S(1)} all-gather(bf16[256,256]{1,0:T(8,128)(2,1)S(1)} %copy-done.3), channel_id=1, replica_groups=mesh['parts'=2,'seq'=4,'head'=2,'fsdp'=2] {'seq'}, dimensions={0}, use_global_device_ids=true | all-gather | bytes 655360 | tf_op jit(solution)/shard_map/all_gather | solution.py:57
  50.8 16.1 %all_gather.36 = bf16[1024,256]{1,0:T(8,128)(2,1)S(1)} all-gather(bf16[256,256]{1,0:T(8,128)(2,1)S(1)} %copy-done.4), channel_id=1, replica_groups=mesh['parts'=2,'seq'=4,'head'=2,'fsdp'=2] {'seq'}, dimensions={0}, use_global_device_ids=true | all-gather | bytes 655360 | tf_op jit(solution)/shard_map/all_gather | solution.py:58
  67.0 0.6 fusion.14
  67.6 14.8 %all_gather.37 = bf16[1024,256]{1,0:T(8,128)(2,1)S(1)} all-gather(bf16[256,256]{1,0:T(8,128)(2,1)S(1)} %get-tuple-element.129), channel_id=1, replica_groups=mesh['parts'=2,'seq'=4,'head'=2,'fsdp'=2] {'seq'}, dimensions={0}, use_global_device_ids=true | all-gather | bytes 655360 | tf_op jit(solution)/shard_map/all_gather | solution.py:82
  82.5 16.1 %all_gather.38 = bf16[1024,256]{1,0:T(8,128)(2,1)S(1)} all-gather(bf16[256,256]{1,0:T(8,128)(2,1)S(1)} %get-tuple-element.127), channel_id=1, replica_groups=mesh['parts'=2,'seq'=4,'head'=2,'fsdp'=2] {'seq'}, dimensions={0}, use_global_device_ids=true | all-gather | bytes 655360 | tf_op jit(solution)/shard_map/all_gather | solution.py:83
  98.8 4.0 %while.15 = (s32[]{:T(128)}, f32[2,256]{1,0:T(2,128)S(1)}, f32[2,256]{1,0:T(2,128)S(1)}, f32[2,256,128]{2,1,0:T(8,128)S(1)}, s32[2,512]{1,0:T(2,128)S(1)}, /*ind...) while((s32[]{:T(128)}, f32[2,256]{1,0:T(2,128)S(1)}, ...), condition=%wide.region_5.6_spmd.clone, body=%wide.region_2.5_spmd.clone.sunk | while | flops 136252416 | bytes 5409925 | solution.py:111
  98.8 0.4 constant_dynamic-slice_fusion.3
  99.1 0.7 compare_reduce_fusion.2
  100.3 0.4 convolution_add_fusion.2
  100.8 0.4 constant_dynamic-slice_fusion.3
  101.2 0.7 compare_reduce_fusion.2
  102.4 0.4 convolution_add_fusion.2
  103.0 15.8 %all_gather.39 = bf16[256,1024]{1,0:T(8,128)(2,1)S(1)} all-gather(bf16[256,256]{1,0:T(8,128)(2,1)S(1)} %copy-done.5), channel_id=1, replica_groups=mesh['parts'=2,'seq'=4,'head'=2,'fsdp'=2] {'seq'}, dimensions={1}, use_global_device_ids=true | all-gather | bytes 655360 | tf_op jit(solution)/shard_map/all_gather | solution.py:63
  118.8 1.1 convolution_convert_fusion.1
  120.7 15.6 %all_gather.42 = bf16[1024,256]{1,0:T(8,128)(2,1)S(1)} all-gather(bf16[256,256]{1,0:T(8,128)(2,1)S(1)} %copy-done.6), channel_id=1, replica_groups=mesh['parts'=2,'seq'=4,'head'=2,'fsdp'=2] {'seq'}, dimensions={0}, use_global_device_ids=true | all-gather | bytes 655360 | tf_op jit(solution)/shard_map/all_gather | solution.py:60
  136.2 15.0 %all_gather.41 = bf16[1024,256]{1,0:T(8,128)(2,1)S(1)} all-gather(bf16[256,256]{1,0:T(8,128)(2,1)S(1)} %copy-done.7), channel_id=1, replica_groups=mesh['parts'=2,'seq'=4,'head'=2,'fsdp'=2] {'seq'}, dimensions={0}, use_global_device_ids=true | all-gather | bytes 655360 | tf_op jit(solution)/shard_map/all_gather | solution.py:59
  151.3 1.0 fusion.37
  152.3 1.1 multiply_reduce_fusion
  153.5 1.0 multiply_convert_fusion.1
  154.5 6.8 %all_gather.40 = bf16[256,1024]{1,0:T(8,128)(2,1)S(1)} all-gather(bf16[64,1024]{1,0:T(8,128)(2,1)S(1)} %multiply_convert_fusion.1), channel_id=1, replica_groups=mesh['parts'=2,'seq'=4,'head'=2,'fsdp'=2] {'head','fsdp'}, dimensions={0}, use_global_device_ids=true | all-gather | bytes 655360 | tf_op jit(solution)/shard_map/all_gather | solution.py:127
  161.3 0.3 fusion.19
  161.9 3.9 %collective-permute-start = (bf16[4,256]{1,0:T(4,128)(2,1)S(1)}, bf16[4,256]{1,0:T(4,128)(2,1)S(1)}, u32[]{:S(2)}, u32[]{:S(2)}) collective-permute-start(bf16[4,256]{1,0:T(4,128)(2,1)S(1)} %get-tuple-element.130), channel_id=1, source_target_pairs={{0,4},{4,8},{8,12},{1,5},{5,9},{9,13},{2,6},{6,10},{10,14},{3,7},{... | collective-permute-start | bytes 6152 | tf_op jit(solution)/shard_map/ppermute | solution.py:16
  165.8 1.3 collective-permute-start.1
  167.2 16.9 %all_gather.43 = bf16[256,1024]{1,0:T(8,128)(2,1)S(1)} all-gather(bf16[256,256]{1,0:T(8,128)(2,1)S(1)} %copy-done.8), channel_id=1, replica_groups=mesh['parts'=2,'seq'=4,'head'=2,'fsdp'=2] {'seq'}, dimensions={1}, use_global_device_ids=true | all-gather | bytes 655360 | tf_op jit(solution)/shard_map/all_gather | solution.py:64
  184.2 1.4 convolution_convert_fusion
  185.5 23.0 %reduce-scatter.5.cloned.1.call-done = bf16[64,1024]{1,0:T(8,128)(2,1)} async-done(((bf16[256,1024]{1,0:T(8,128)(2,1)}), bf16[64,1024]{1,0:T(8,128)(2,1)}) %reduce-scatter.5.cloned.1.call-update) | async-done | bytes 131088 | tf_op jit(solution)/shard_map/reduce_scatter | solution.py:141
  208.5 1.6 add_convert_fusion
  (62 shorter events, 2.0 us)
Async XLA Ops:
  6.5 12.0 %copy-start.2 = (bf16[256,256]{1,0:T(8,128)(2,1)S(1)}, bf16[256,256]{1,0:T(8,128)(2,1)}, u32[]{:S(2)}) copy-start(bf16[256,256]{1,0:T(8,128)(2,1)} %param.19) | copy-start | bytes 393220
  6.5 28.4 %copy-start.3 = (bf16[256,256]{1,0:T(8,128)(2,1)S(1)}, bf16[256,256]{1,0:T(8,128)(2,1)}, u32[]{:S(2)}) copy-start(bf16[256,256]{1,0:T(8,128)(2,1)} %param.20) | copy-start | bytes 393220
  6.5 144.7 %reduce-scatter.3.cloned.1.call-start = ((), (), s32[]{:S(2)}) async-start(), calls=%async_computation.2 | async-start | bytes 655360 | tf_op jit(solution)/shard_map/reduce_scatter | solution.py:119
  9.8 41.0 %copy-start.4 = (bf16[256,256]{1,0:T(8,128)(2,1)S(1)}, bf16[256,256]{1,0:T(8,128)(2,1)}, u32[]{:S(2)}) copy-start(bf16[256,256]{1,0:T(8,128)(2,1)} %param.21) | copy-start | bytes 393220
  98.7 4.2 %copy-start.5 = (bf16[256,256]{1,0:T(8,128)(2,1)S(1)}, bf16[256,256]{1,0:T(8,128)(2,1)}, u32[]{:S(2)}) copy-start(bf16[256,256]{1,0:T(8,128)(2,1)} %param.22) | copy-start | bytes 393220
  118.8 1.9 copy-start.6
  118.8 17.4 %copy-start.7 = (bf16[256,256]{1,0:T(8,128)(2,1)S(1)}, bf16[256,256]{1,0:T(8,128)(2,1)}, u32[]{:S(2)}) copy-start(bf16[256,256]{1,0:T(8,128)(2,1)} %param.24) | copy-start | bytes 393220
  119.9 31.3 %copy-start.9 = (f32[9,256]{1,0:T(8,128)S(1)}, f32[9,256]{1,0:T(8,128)}, u32[]{:S(2)}) copy-start(f32[9,256]{1,0:T(8,128)} %param.26) | copy-start | bytes 27652
  119.9 31.3 %copy-start = (bf16[64,1024]{1,0:T(8,128)(2,1)S(1)}, bf16[64,1024]{1,0:T(8,128)(2,1)}, u32[]{:S(2)}) copy-start(bf16[64,1024]{1,0:T(8,128)(2,1)} %param.16) | copy-start | bytes 393220
  120.0 33.5 %copy-start.10 = (f32[1024]{0:T(1024)S(1)}, f32[1024]{0:T(1024)}, u32[]{:S(2)}) copy-start(f32[1024]{0:T(1024)} %param.23) | copy-start | bytes 12292
  120.0 88.6 %reduce-scatter.5.cloned.1.call-start = ((), (), s32[]{:S(2)}) async-start(), calls=%async_computation.3 | async-start | bytes 655360 | tf_op jit(solution)/shard_map/reduce_scatter | solution.py:141
  161.6 5.6 %copy-start.8 = (bf16[256,256]{1,0:T(8,128)(2,1)S(1)}, bf16[256,256]{1,0:T(8,128)(2,1)}, u32[]{:S(2)}) copy-start(bf16[256,256]{1,0:T(8,128)(2,1)} %param.29) | copy-start | bytes 393220
  161.6 22.5 %copy-start.11 = (f32[256]{0:T(256)S(1)}, f32[256]{0:T(256)}, u32[]{:S(2)}) copy-start(f32[256]{0:T(256)} %param.28) | copy-start | bytes 3076
  161.6 22.5 %copy-start.12 = (f32[256]{0:T(256)S(1)}, f32[256]{0:T(256)}, u32[]{:S(2)}) copy-start(f32[256]{0:T(256)} %param.27) | copy-start | bytes 3076
  161.9 22.2 %collective-permute-start = (bf16[4,256]{1,0:T(4,128)(2,1)S(1)}, bf16[4,256]{1,0:T(4,128)(2,1)S(1)}, u32[]{:S(2)}, u32[]{:S(2)}) collective-permute-start(bf16[4,256]{1,0:T(4,128)(2,1)S(1)} %get-tuple-element.130), channel_id=1, source_target_pairs={{0,4},{4,8},{8,12},{1,5},{5,9},{9,13},{2,6},{6,10},{10,14},{3,7},{... | collective-permute-start | bytes 6152 | tf_op jit(solution)/shard_map/ppermute | solution.py:16
  165.8 18.3 %collective-permute-start.1 = (bf16[4,256]{1,0:T(4,128)(2,1)S(1)}, bf16[4,256]{1,0:T(4,128)(2,1)S(1)}, u32[]{:S(2)}, u32[]{:S(2)}) collective-permute-start(bf16[4,256]{1,0:T(4,128)(2,1)S(1)} %get-tuple-element.131), channel_id=1, source_target_pairs={{4,0},{8,4},{12,8},{5,1},{9,5},{13,9},{6,2},{10,6},{14,10},{7,3},{... | collective-permute-start | bytes 6152 | tf_op jit(solution)/shard_map/ppermute | solution.py:19
  184.2 24.4 %copy-start.1 = (bf16[64,1024]{1,0:T(8,128)(2,1)S(1)}, bf16[64,1024]{1,0:T(8,128)(2,1)}, u32[]{:S(2)}) copy-start(bf16[64,1024]{1,0:T(8,128)(2,1)} %reduce-scatter.3.cloned.1.call-done) | copy-start | bytes 393220
Sparse Core Ops, SparseCore 0:
  120.1 22.2 reduce-scatter.2
  185.7 22.8 reduce-scatter.4
where the time goes:
time: 217 us
  blocking collectives  158 us (73%)
  waiting for transfers between devices  23 us (11%)
  between operations  14.4 us (7%)
  other arithmetic  9.78 us (5%)
  starting transfers between devices  5.23 us (2%)
  matrix products  5.13 us (2%)
    reduce_scatter x1, waiting for transfers between devices, shards(): lax.psum_scatter(jnp.dot(active, down_rows, preferred_element_type=jnp.fl...  23 us
    all_gather x1, blocking collectives, shards(): lax.all_gather(pw2, 'seq', axis=1, tiled=True)  16.9 us
    all_gather x1, blocking collectives, shards(): lax.all_gather(w_query, 'seq', axis=0, tiled=True)  16.3 us
    all_gather x1, blocking collectives, shards(): lax.all_gather(w_value, 'seq', axis=0, tiled=True)  16.1 us
    all_gather x1, blocking collectives, shards(): value_piece = lax.all_gather(values_here, 'seq', axis=0, tiled=True)  16.1 us
    all_gather x1, blocking collectives, shards(): lax.all_gather(w_key, 'seq', axis=0, tiled=True)  15.9 us
    all_gather x1, blocking collectives, shards(): lax.all_gather(w_out, 'seq', axis=1, tiled=True)  15.8 us
    all_gather x1, blocking collectives, shards(): lax.all_gather(pw1_gate, 'seq', axis=0, tiled=True)  15.6 us
  transfers between devices with their start and end apart: 4, of which 1 were waited for; matrix products, arithmetic and copies ran while one was open for 0% of the time, Pallas kernels for 0%

commit v1 on v0

--- a/solution.py
+++ b/solution.py
@@ -79,8 +79,13 @@
         jnp.zeros((heads_here, block_rows), jnp.float32),
         jnp.zeros((heads_here, block_rows, HD), jnp.float32),
     )
-    key_piece = lax.all_gather(keys_here, "seq", axis=0, tiled=True)
-    value_piece = lax.all_gather(values_here, "seq", axis=0, tiled=True)
+    key_piece, value_piece = jnp.split(
+        lax.all_gather(
+            jnp.concatenate([keys_here, values_here], axis=1), "seq", axis=0, tiled=True
+        ),
+        [keys_here.shape[1]],
+        axis=1,
+    )
     row_count = key_piece.shape[0]
     block_size = math.gcd(row_count, 512)
     block_count = row_count // block_size

time: 217 us -> 201 us (0.926)
  blocking collectives: 158 us -> 129 us
  waiting for transfers between devices: 23 us -> 36.7 us
  starting transfers between devices: 5.23 us -> 2.67 us
    all_gather x2 -> x0, blocking collectives: 30.9 us -> none  [the longest x1 16.1 us: shards(): value_piece = lax.all_gather(values_here, 'seq', axis=0, tiled=True)]
    all_gather x0 -> x1, waiting for transfers between devices: none -> 13.6 us  [shards(): lax.all_gather(jnp.concatenate([keys_here, values_here], axis=1), 'seq',...]
    ppermute x1, starting transfers between devices: 3.9 us -> 1.29 us  [with_halo(): lax.ppermute(lax.slice_in_dim(block, block.shape[dim] - width, None, axis...]
  transfers between devices with their start and end apart: 4 -> 5, of which waited for: 1 -> 2; matrix products, arithmetic and copies ran while one was open for 0% -> 0% of each run, Pallas kernels for 0% -> 0%
where the time goes in v1:
time: 201 us; the launch traced here: 200 us
  blocking collectives  129 us (64%)
  waiting for transfers between devices  36.7 us (18%)
  between operations  14.1 us (7%)
  other arithmetic  9.77 us (5%)
  matrix products  5.17 us (3%)
  local copies, waits for them, and re-layouts  3.19 us (2%)
  starting transfers between devices  2.67 us (1%)
    reduce_scatter x1, waiting for transfers between devices, shards(): lax.psum_scatter(jnp.dot(active, down_rows, preferred_element_type=jnp.fl...  23 us
    all_gather x1, blocking collectives, shards(): lax.all_gather(w_out, 'seq', axis=1, tiled=True)  17.1 us
    all_gather x1, blocking collectives, shards(): lax.all_gather(pw2, 'seq', axis=1, tiled=True)  16.6 us
    all_gather x1, blocking collectives, shards(): lax.all_gather(w_query, 'seq', axis=0, tiled=True)  16.3 us
    all_gather x1, blocking collectives, shards(): lax.all_gather(pw1_gate, 'seq', axis=0, tiled=True)  16.2 us
    all_gather x1, blocking collectives, shards(): lax.all_gather(w_value, 'seq', axis=0, tiled=True)  16.1 us
    all_gather x1, blocking collectives, shards(): lax.all_gather(w_key, 'seq', axis=0, tiled=True)  15.9 us
    all_gather x1, blocking collectives, shards(): lax.all_gather(pw1_value, 'seq', axis=0, tiled=True)  15 us
  transfers between devices with their start and end apart: 5, of which 2 were waited for; matrix products, arithmetic and copies ran while one was open for 0% of the time, Pallas kernels for 0%

profile of v1, /device:TPU:0, one launch (start us, length us, event | category | flops | bytes accessed | tf_op | source)
XLA Modules:
  0.0 200.5 jit_solution(17257348557183848073)
XLA Ops:
  6.5 1.1 convert_reduce_fusion
  7.6 1.1 fusion.24
  8.7 1.0 fusion.26
  9.8 8.8 %all_gather.30 = bf16[256,1024]{1,0:T(8,128)(2,1)S(1)} all-gather(bf16[64,1024]{1,0:T(8,128)(2,1)S(1)} %fusion.26), channel_id=1, replica_groups=mesh['parts'=2,'seq'=4,'head'=2,'fsdp'=2] {'head','fsdp'}, dimensions={0}, use_global_device_ids=true | all-gather | bytes 655360 | tf_op jit(solution)/shard_map/all_gather | solution.py:70
  18.5 16.3 %all_gather.31 = bf16[1024,256]{1,0:T(8,128)(2,1)S(1)} all-gather(bf16[256,256]{1,0:T(8,128)(2,1)S(1)} %copy-done.2), channel_id=1, replica_groups=mesh['parts'=2,'seq'=4,'head'=2,'fsdp'=2] {'seq'}, dimensions={0}, use_global_device_ids=true | all-gather | bytes 655360 | tf_op jit(solution)/shard_map/all_gather | solution.py:56
  34.9 15.9 %all_gather.32 = bf16[1024,256]{1,0:T(8,128)(2,1)S(1)} all-gather(bf16[256,256]{1,0:T(8,128)(2,1)S(1)} %copy-done.3), channel_id=1, replica_groups=mesh['parts'=2,'seq'=4,'head'=2,'fsdp'=2] {'seq'}, dimensions={0}, use_global_device_ids=true | all-gather | bytes 655360 | tf_op jit(solution)/shard_map/all_gather | solution.py:57
  50.8 16.1 %all_gather.33 = bf16[1024,256]{1,0:T(8,128)(2,1)S(1)} all-gather(bf16[256,256]{1,0:T(8,128)(2,1)S(1)} %copy-done.4), channel_id=1, replica_groups=mesh['parts'=2,'seq'=4,'head'=2,'fsdp'=2] {'seq'}, dimensions={0}, use_global_device_ids=true | all-gather | bytes 655360 | tf_op jit(solution)/shard_map/all_gather | solution.py:58
  66.9 0.6 fusion.14
  67.5 0.7 concatenate.12
  68.4 17.1 %all_gather.35 = bf16[256,1024]{1,0:T(8,128)(2,1)S(1)} all-gather(bf16[256,256]{1,0:T(8,128)(2,1)S(1)} %copy-done.5), channel_id=1, replica_groups=mesh['parts'=2,'seq'=4,'head'=2,'fsdp'=2] {'seq'}, dimensions={1}, use_global_device_ids=true | all-gather | bytes 655360 | tf_op jit(solution)/shard_map/all_gather | solution.py:63
  85.4 13.6 %all-gather.2.cloned.1.call-done = bf16[1024,512]{1,0:T(8,128)(2,1)} async-done(((bf16[256,512]{1,0:T(8,128)(2,1)}), bf16[1024,512]{1,0:T(8,128)(2,1)}) %all-gather.2.cloned.1.call-update) | async-done | bytes 1048592 | tf_op jit(solution)/shard_map/all_gather | solution.py:83
  99.0 1.3 fusion.41
  100.6 4.0 %while.15 = (s32[]{:T(128)}, f32[2,256]{1,0:T(2,128)S(1)}, f32[2,256]{1,0:T(2,128)S(1)}, f32[2,256,128]{2,1,0:T(8,128)S(1)}, s32[2,512]{1,0:T(2,128)S(1)}, /*ind...) while((s32[]{:T(128)}, f32[2,256]{1,0:T(2,128)S(1)}, ...), condition=%wide.region_5.6_spmd.clone, body=%wide.region_2.5_spmd.clone.sunk | while | flops 136252416 | bytes 5409925 | solution.py:116
  100.6 0.4 constant_dynamic-slice_fusion.3
  101.0 0.7 compare_reduce_fusion.2
  102.2 0.4 convolution_add_fusion.2
  102.6 0.4 constant_dynamic-slice_fusion.3
  103.0 0.7 compare_reduce_fusion.2
  104.2 0.4 convolution_add_fusion.2
  104.8 1.1 convolution_convert_fusion.1
  106.7 16.2 %all_gather.38 = bf16[1024,256]{1,0:T(8,128)(2,1)S(1)} all-gather(bf16[256,256]{1,0:T(8,128)(2,1)S(1)} %copy-done.6), channel_id=1, replica_groups=mesh['parts'=2,'seq'=4,'head'=2,'fsdp'=2] {'seq'}, dimensions={0}, use_global_device_ids=true | all-gather | bytes 655360 | tf_op jit(solution)/shard_map/all_gather | solution.py:60
  122.9 15.0 %all_gather.37 = bf16[1024,256]{1,0:T(8,128)(2,1)S(1)} all-gather(bf16[256,256]{1,0:T(8,128)(2,1)S(1)} %copy-done.7), channel_id=1, replica_groups=mesh['parts'=2,'seq'=4,'head'=2,'fsdp'=2] {'seq'}, dimensions={0}, use_global_device_ids=true | all-gather | bytes 655360 | tf_op jit(solution)/shard_map/all_gather | solution.py:59
  138.0 1.0 fusion.37
  139.1 1.1 multiply_reduce_fusion
  140.2 1.0 multiply_convert_fusion.1
  141.2 6.7 %all_gather.36 = bf16[256,1024]{1,0:T(8,128)(2,1)S(1)} all-gather(bf16[64,1024]{1,0:T(8,128)(2,1)S(1)} %multiply_convert_fusion.1), channel_id=1, replica_groups=mesh['parts'=2,'seq'=4,'head'=2,'fsdp'=2] {'head','fsdp'}, dimensions={0}, use_global_device_ids=true | all-gather | bytes 655360 | tf_op jit(solution)/shard_map/all_gather | solution.py:132
  148.6 1.3 collective-permute-start
  149.9 1.3 collective-permute-start.1
  151.2 16.6 %all_gather.39 = bf16[256,1024]{1,0:T(8,128)(2,1)S(1)} all-gather(bf16[256,256]{1,0:T(8,128)(2,1)S(1)} %copy-done.8), channel_id=1, replica_groups=mesh['parts'=2,'seq'=4,'head'=2,'fsdp'=2] {'seq'}, dimensions={1}, use_global_device_ids=true | all-gather | bytes 655360 | tf_op jit(solution)/shard_map/all_gather | solution.py:64
  167.9 1.4 convolution_convert_fusion
  169.3 23.0 %reduce-scatter.5.cloned.1.call-done = bf16[64,1024]{1,0:T(8,128)(2,1)} async-done(((bf16[256,1024]{1,0:T(8,128)(2,1)}), bf16[64,1024]{1,0:T(8,128)(2,1)}) %reduce-scatter.5.cloned.1.call-update) | async-done | bytes 131088 | tf_op jit(solution)/shard_map/reduce_scatter | solution.py:146
  192.3 1.6 add_convert_fusion
  (64 shorter events, 2.4 us)
Async XLA Ops:
  6.5 12.0 %copy-start.2 = (bf16[256,256]{1,0:T(8,128)(2,1)S(1)}, bf16[256,256]{1,0:T(8,128)(2,1)}, u32[]{:S(2)}) copy-start(bf16[256,256]{1,0:T(8,128)(2,1)} %param.19) | copy-start | bytes 393220
  6.5 28.3 %copy-start.3 = (bf16[256,256]{1,0:T(8,128)(2,1)S(1)}, bf16[256,256]{1,0:T(8,128)(2,1)}, u32[]{:S(2)}) copy-start(bf16[256,256]{1,0:T(8,128)(2,1)} %param.20) | copy-start | bytes 393220
  6.5 92.5 %all-gather.2.cloned.1.call-start = ((), (), s32[]{:S(2)}) async-start(), calls=%async_computation.2 | async-start | bytes 1310720 | tf_op jit(solution)/shard_map/all_gather | solution.py:83
  9.8 41.0 %copy-start.4 = (bf16[256,256]{1,0:T(8,128)(2,1)S(1)}, bf16[256,256]{1,0:T(8,128)(2,1)}, u32[]{:S(2)}) copy-start(bf16[256,256]{1,0:T(8,128)(2,1)} %param.21) | copy-start | bytes 393220
  66.9 1.4 copy-start.5
  68.3 69.7 %reduce-scatter.3.cloned.1.call-start = ((), (), s32[]{:S(2)}) async-start(), calls=%async_computation.3 | async-start | bytes 655360 | tf_op jit(solution)/shard_map/reduce_scatter | solution.py:124
  104.8 1.9 copy-start.6
  104.8 18.1 %copy-start.7 = (bf16[256,256]{1,0:T(8,128)(2,1)S(1)}, bf16[256,256]{1,0:T(8,128)(2,1)}, u32[]{:S(2)}) copy-start(bf16[256,256]{1,0:T(8,128)(2,1)} %param.24) | copy-start | bytes 393220
  106.0 32.0 %copy-start.9 = (f32[9,256]{1,0:T(8,128)S(1)}, f32[9,256]{1,0:T(8,128)}, u32[]{:S(2)}) copy-start(f32[9,256]{1,0:T(8,128)} %param.26) | copy-start | bytes 27652
  106.0 32.0 %copy-start = (bf16[64,1024]{1,0:T(8,128)(2,1)S(1)}, bf16[64,1024]{1,0:T(8,128)(2,1)}, u32[]{:S(2)}) copy-start(bf16[64,1024]{1,0:T(8,128)(2,1)} %param.16) | copy-start | bytes 393220
  106.0 34.2 %copy-start.10 = (f32[1024]{0:T(1024)S(1)}, f32[1024]{0:T(1024)}, u32[]{:S(2)}) copy-start(f32[1024]{0:T(1024)} %param.23) | copy-start | bytes 12292
  106.0 86.3 %reduce-scatter.5.cloned.1.call-start = ((), (), s32[]{:S(2)}) async-start(), calls=%async_computation.4 | async-start | bytes 655360 | tf_op jit(solution)/shard_map/reduce_scatter | solution.py:146
  148.3 3.0 %copy-start.8 = (bf16[256,256]{1,0:T(8,128)(2,1)S(1)}, bf16[256,256]{1,0:T(8,128)(2,1)}, u32[]{:S(2)}) copy-start(bf16[256,256]{1,0:T(8,128)(2,1)} %param.29) | copy-start | bytes 393220
  148.3 19.6 %copy-start.11 = (f32[256]{0:T(256)S(1)}, f32[256]{0:T(256)}, u32[]{:S(2)}) copy-start(f32[256]{0:T(256)} %param.28) | copy-start | bytes 3076
  148.3 19.6 %copy-start.12 = (f32[256]{0:T(256)S(1)}, f32[256]{0:T(256)}, u32[]{:S(2)}) copy-start(f32[256]{0:T(256)} %param.27) | copy-start | bytes 3076
  148.6 19.2 %collective-permute-start = (bf16[4,256]{1,0:T(4,128)(2,1)S(1)}, bf16[4,256]{1,0:T(4,128)(2,1)S(1)}, u32[]{:S(2)}, u32[]{:S(2)}) collective-permute-start(bf16[4,256]{1,0:T(4,128)(2,1)S(1)} %get-tuple-element.129), channel_id=1, source_target_pairs={{0,4},{4,8},{8,12},{1,5},{5,9},{9,13},{2,6},{6,10},{10,14},{3,7},{... | collective-permute-start | bytes 6152 | tf_op jit(solution)/shard_map/ppermute | solution.py:16
  149.9 17.9 %collective-permute-start.1 = (bf16[4,256]{1,0:T(4,128)(2,1)S(1)}, bf16[4,256]{1,0:T(4,128)(2,1)S(1)}, u32[]{:S(2)}, u32[]{:S(2)}) collective-permute-start(bf16[4,256]{1,0:T(4,128)(2,1)S(1)} %get-tuple-element.130), channel_id=1, source_target_pairs={{4,0},{8,4},{12,8},{5,1},{9,5},{13,9},{6,2},{10,6},{14,10},{7,3},{... | collective-permute-start | bytes 6152 | tf_op jit(solution)/shard_map/ppermute | solution.py:19
  167.9 24.4 %copy-start.1 = (bf16[64,1024]{1,0:T(8,128)(2,1)S(1)}, bf16[64,1024]{1,0:T(8,128)(2,1)}, u32[]{:S(2)}) copy-start(bf16[64,1024]{1,0:T(8,128)(2,1)} %reduce-scatter.3.cloned.1.call-done) | copy-start | bytes 393220
Sparse Core Ops, SparseCore 0:
  68.4 30.6 all-gather.1
  106.1 20.2 reduce-scatter.2
  169.4 22.8 reduce-scatter.4
